TPU v7x, 128 devices: a whole 4x4x4 slice. The times are simulated.
128 devices in a mesh: wide: 16 (over y, x), narrow: 8 (over z, core).
Axes of the slice: x: 4, y: 4, z: 4, core: 2. Of those that a mesh axis runs over, the one named last changes fastest.
Arguments:
- tokens: bfloat16 [256, 128, 1536], P('wide'), may hold values from -8 to 8
- ln_gain: bfloat16 [1536], replicated, may hold values from 0.3984375 to 1.59375
- gate_weight: bfloat16 [1536, 8960], P(None, 'narrow'), may hold values from -0.15625 to 0.15625
- up_weight: bfloat16 [1536, 8960], P(None, 'narrow'), may hold values from -0.15625 to 0.15625
- down_weight: bfloat16 [8960, 1536], P('narrow'), may hold values from -0.0625 to 0.0625
- out_gain: bfloat16 [1536], replicated, may hold values from 0.25 to 1.75
- shard_ids: int32 [256], P('wide'), may hold values from 0 to 15, as said below
- slab_old: bfloat16 [262144, 1536], P(('wide', 'narrow')), may hold values from -8 to 8
- queries: bfloat16 [16, 64, 1536], P('wide'), may hold values from -12 to 12
- positives: int32 [16, 64], P('wide'), may hold values from 0 to 262399
- owners: int32 [4], replicated, may hold values from 0 to 15
Outputs:
- index_new: bfloat16 [16, 16, 2, 1536], P('wide', 'narrow')
- losses: float32 [4, 64], replicated
Inputs may be any that keep to these rules, and one draw needn't show every extreme that they name: `shard_ids`: among the 16 passages of one index of wide at most 2 have the same shard id; in every draw one shard id is held by exactly 2 passages of every index of wide.
All inputs are finite; a program needn't handle non-finite values.
Results may differ from a plain program's by a relative error of at most 0.0029.
Values may be sent and summed in bfloat16 or wider, within the bound.
No kernel may reach another device: no remote copies, remote signals or barrier semaphores. Data moves between devices by JAX's collectives and lax.ppermute only.
A program may use at most 128 MiB of HBM per device.

v0:
```python
import math
import jax
import jax.numpy as jnp
from jax import lax
from jax.sharding import PartitionSpec as P

EPS = 1e-06


def spread(x, axis, root):
    mine = lax.axis_index(axis) == root
    return lax.psum(jnp.where(mine, x, jnp.zeros_like(x)), axis)


def rms_scale(values):
    return lax.rsqrt(jnp.mean(values * values, axis=-1, keepdims=True) + EPS)


def local(
    tokens,
    ln_gain,
    gate_weight,
    up_weight,
    down_weight,
    out_gain,
    shard_ids,
    slab_old,
    queries,
    positives,
    owners,
):
    passages, seq_len, width = tokens.shape
    narrow_count = lax.axis_size("narrow")
    wide_count = lax.axis_size("wide")
    narrow_rank = lax.axis_index("narrow")
    wide_rank = lax.axis_index("wide")
    piece_width = width // narrow_count
    capacity = 2 * passages // wide_count
    values = tokens.astype(jnp.float32)
    normed = (values * rms_scale(values) * ln_gain.astype(jnp.float32)).astype(jnp.bfloat16)
    normed = normed.reshape(passages * seq_len, width)
    gate = jnp.dot(normed, gate_weight, preferred_element_type=jnp.float32)
    upward = jnp.dot(normed, up_weight, preferred_element_type=jnp.float32)
    hidden = (jax.nn.silu(gate) * upward).astype(jnp.bfloat16)
    partial_value = jnp.dot(hidden, down_weight, preferred_element_type=jnp.float32)
    pooled_part = jnp.mean(partial_value.reshape(passages, seq_len, width), axis=1)
    token_mean = jnp.mean(values, axis=1)
    offset = narrow_rank * piece_width
    pooled = lax.psum(pooled_part, "narrow") + token_mean
    norm_scale = rms_scale(pooled)
    own_piece = lax.dynamic_slice_in_dim(pooled, offset, piece_width, 1)
    gain_piece = lax.dynamic_slice_in_dim(out_gain.astype(jnp.float32), offset, piece_width, 0)
    embedding = (own_piece * norm_scale * gain_piece).astype(jnp.bfloat16)
    positions = jnp.arange(passages, dtype=jnp.int32)
    earlier = positions[:, None] > positions[None, :]
    same = shard_ids[:, None] == shard_ids[None, :]
    rank = jnp.sum((earlier & same).astype(jnp.int32), axis=1)
    slots = shard_ids * capacity + rank
    dispatch = slots[None, :] == jnp.arange(wide_count * capacity, dtype=jnp.int32)[:, None]
    outgoing = jnp.dot(dispatch.astype(jnp.bfloat16), embedding, preferred_element_type=jnp.float32)
    outgoing = outgoing.astype(jnp.bfloat16).reshape(wide_count, capacity, piece_width)
    numbers = wide_rank * passages + positions
    slot_numbers = jnp.sum(jnp.where(dispatch, numbers[None, :] + 1, 0), axis=1) - 1
    slot_numbers = slot_numbers.reshape(wide_count, capacity, 1)
    arrived, arrived_numbers = (
        lax.all_to_all(
            lax.all_to_all(outgoing, "wide", split_axis=0, concat_axis=0, tiled=True),
            "narrow",
            split_axis=0,
            concat_axis=2,
            tiled=True,
        ),
        lax.all_to_all(
            lax.all_to_all(slot_numbers, "wide", split_axis=0, concat_axis=0, tiled=True),
            "narrow",
            split_axis=0,
            concat_axis=2,
            tiled=True,
        ),
    )
    old_total = slab_old.shape[0] * wide_count * narrow_count
    new_rows = arrived.reshape(-1, width)
    new_numbers = arrived_numbers[:, :, 0].reshape(-1)
    valid = (new_numbers >= 0)[None, :]
    new_global = old_total + new_numbers
    device_linear = wide_rank * narrow_count + narrow_rank
    old_global = device_linear * slab_old.shape[0] + jnp.arange(slab_old.shape[0], dtype=jnp.int32)
    scale = 1.0 / math.sqrt(width)
    contract = (((1,), (1,)), ((), ()))
    block_size = queries.shape[1]
    step_count = owners.shape[0]

    def score_rows(block, positive):
        old_scores = (
            lax.dot_general(block, slab_old, contract, preferred_element_type=jnp.float32) * scale
        )
        new_scores = (
            lax.dot_general(block, new_rows, contract, preferred_element_type=jnp.float32) * scale
        )
        masked = jnp.where(valid, new_scores, -jnp.inf)
        local_max = jnp.maximum(jnp.max(old_scores, axis=1), jnp.max(masked, axis=1))
        hit_old = old_global[None, :] == positive[:, None]
        hit_new = valid & (new_global[None, :] == positive[:, None])
        local_positive = jnp.sum(jnp.where(hit_old, old_scores, 0.0), axis=1) + jnp.sum(
            jnp.where(hit_new, new_scores, 0.0), axis=1
        )
        largest = lax.pmax(local_max, ("wide", "narrow"))
        local_total = jnp.sum(jnp.exp(old_scores - largest[:, None]), axis=1)
        local_total = local_total + jnp.sum(
            jnp.where(valid, jnp.exp(new_scores - largest[:, None]), 0.0), axis=1
        )
        total, picked = lax.psum((local_total, local_positive), ("wide", "narrow"))
        return largest + jnp.log(total) - picked

    def step_body(step, losses):
        owner = owners[step]
        block, positive = (spread(queries[0], "wide", owner), spread(positives[0], "wide", owner))
        loss = score_rows(block, positive)
        return lax.dynamic_update_slice_in_dim(losses, loss[None, :], step, 0)

    start_losses = jnp.zeros((step_count, block_size), jnp.float32)
    losses = lax.fori_loop(0, step_count, step_body, start_losses)
    return (arrived[None], losses)


def solution(mesh):
    return jax.shard_map(
        local,
        mesh=mesh,
        in_specs=(
            P("wide", None, None),
            P(),
            P(None, "narrow"),
            P(None, "narrow"),
            P("narrow", None),
            P(),
            P("wide"),
            P(("wide", "narrow"), None),
            P("wide", None, None),
            P("wide", None),
            P(),
        ),
        out_specs=(P("wide", "narrow", None, None), P()),
        check_vma=False,
    )
```

profile of v0, /device:TPU:1, one launch (start us, length us, event | category | flops | bytes accessed | tf_op | source)
XLA Modules:
  0.0 1026.5 jit_solution(8330299875181176620)
XLA Ops:
  8.1 4.9 convert_reduce_fusion
  13.0 1.5 fusion.5
  14.5 2.7 copy-done.2
  17.2 9.7 fusion.16
  26.9 22.3 %bitcast_reduce_fusion = f32[16,1536]{1,0:T(8,128)} fusion(bf16[1120,1536]{1,0:T(8,128)(2,1)} %param.17, bf16[2048,1536]{1,0:T(8,128)(2,1)} %bitcast.51, bf16[1536,1120]{0,1:T(8,128)(2,1)} %param.16, f32[2048,1120]{0,1:T(8,128)} %fusion.16), kind=kOutput, calls=%fused_computation.19 | convolution fusion | flops 14109745152 | bytes 22446080 | tf_op jit(solution)/shard_map/dot_general | solution.py:45
  49.2 1.5 broadcast_multiply_fusion
  51.8 7.6 all-to-all-start.2
  59.4 1.4 dynamic-slice_convert_fusion
  60.8 4.9 all-to-all-done.2
  65.7 7.6 all-to-all-start.3
  73.2 4.6 all-to-all-done.3
  78.1 32.4 %all-reduce.6.cloned.1.call-done = f32[16,1536]{1,0:T(8,128)} async-done(((f32[16,1536]{1,0:T(8,128)}), f32[16,1536]{1,0:T(8,128)}) %all-reduce.6.cloned.1.call-update) | async-done | bytes 98320 | tf_op jit(solution)/shard_map/psum | solution.py:49
  113.1 6.6 all-to-all-start
  119.8 6.3 all-to-all-done
  126.2 7.2 all-to-all-start.1
  133.6 4.4 all-to-all-done.1
  138.8 881.1 %while.14 = (s32[]{:T(128)}, f32[4,64]{1,0:T(4,128)}, s32[4]{0:T(128)}, bf16[1,64,1536]{2,1,0:T(8,128)(2,1)}, bf16[2048,1536]{1,0:T(8,128)(2,1)}, /*index=5*/pre...) while((s32[]{:T(128)}, f32[4,64]{1,0:T(4,128)}, ...), condition=%wide.region_19.20_spmd.clone, body=%wide.region_7.19_spmd.clone.sunk | while | flops 404558592 | bytes 10132520 | solution.py:122
  138.9 1.3 dynamic_slice.21
  141.6 9.3 psum.59
  150.9 69.7 %all-reduce.8.cloned.1.call-done = bf16[64,1536]{1,0:T(8,128)(2,1)} async-done(((bf16[64,1536]{1,0:T(8,128)(2,1)}), bf16[64,1536]{1,0:T(8,128)(2,1)}) %all-reduce.8.cloned.1.call-update) | async-done | bytes 196624 | tf_op jit(solution)/shard_map/while/body/eval_jaxpr/psum | solution.py:12
  220.6 5.8 fusion.36
  226.6 66.3 %pmax.13 = f32[64]{0:T(128)S(1)} all-reduce(f32[64]{0:T(128)S(1)} %max.11), channel_id=1, replica_groups=mesh['wide'=16,'narrow'=8] {'wide','narrow'}, use_global_device_ids=true, to_apply=%region_11.11 | all-reduce | flops 64 | bytes 512 | tf_op jit(solution)/shard_map/while/body/eval_jaxpr/pmax | solution.py:107
  293.0 1.3 exponential_reduce_fusion.2
  294.4 62.5 %all-reduce.2 = (f32[64]{0:T(128)S(1)}, f32[64]{0:T(128)S(1)}) all-reduce(f32[64]{0:T(128)S(1)} %add.187, f32[64]{0:T(128)S(1)} %add.188), channel_id=1, replica_groups=mesh['wide'=16,'narrow'=8] {'wide','narrow'}, use_global_device_ids=true, to_apply=%region_18.18 | all-reduce | flops 128 | bytes 1024 | tf_op jit(solution)/shard_map/while/body/eval_jaxpr/psum | solution.py:112
  356.9 1.3 dynamic_update_slice.9
  358.2 1.3 dynamic_slice.21
  361.0 10.9 %psum.59 = s32[64]{0:T(128)S(1)} all-reduce(s32[64]{0:T(128)S(1)} %fusion.37), channel_id=1, replica_groups=mesh['wide'=16,'narrow'=8] {'wide'}, use_global_device_ids=true, to_apply=%region_15.15 | all-reduce | flops 64 | bytes 512 | tf_op jit(solution)/shard_map/while/body/eval_jaxpr/psum | solution.py:12
  371.8 69.6 %all-reduce.8.cloned.1.call-done = bf16[64,1536]{1,0:T(8,128)(2,1)} async-done(((bf16[64,1536]{1,0:T(8,128)(2,1)}), bf16[64,1536]{1,0:T(8,128)(2,1)}) %all-reduce.8.cloned.1.call-update) | async-done | bytes 196624 | tf_op jit(solution)/shard_map/while/body/eval_jaxpr/psum | solution.py:12
  441.4 5.8 fusion.36
  447.4 66.4 %pmax.13 = f32[64]{0:T(128)S(1)} all-reduce(f32[64]{0:T(128)S(1)} %max.11), channel_id=1, replica_groups=mesh['wide'=16,'narrow'=8] {'wide','narrow'}, use_global_device_ids=true, to_apply=%region_11.11 | all-reduce | flops 64 | bytes 512 | tf_op jit(solution)/shard_map/while/body/eval_jaxpr/pmax | solution.py:107
  513.8 1.3 exponential_reduce_fusion.2
  515.2 62.5 %all-reduce.2 = (f32[64]{0:T(128)S(1)}, f32[64]{0:T(128)S(1)}) all-reduce(f32[64]{0:T(128)S(1)} %add.187, f32[64]{0:T(128)S(1)} %add.188), channel_id=1, replica_groups=mesh['wide'=16,'narrow'=8] {'wide','narrow'}, use_global_device_ids=true, to_apply=%region_18.18 | all-reduce | flops 128 | bytes 1024 | tf_op jit(solution)/shard_map/while/body/eval_jaxpr/psum | solution.py:112
  577.7 1.3 dynamic_update_slice.9
  579.0 1.3 dynamic_slice.21
  581.0 1.6 select_bitcast_fusion.2
  583.3 9.0 psum.59
  592.3 69.5 %all-reduce.8.cloned.1.call-done = bf16[64,1536]{1,0:T(8,128)(2,1)} async-done(((bf16[64,1536]{1,0:T(8,128)(2,1)}), bf16[64,1536]{1,0:T(8,128)(2,1)}) %all-reduce.8.cloned.1.call-update) | async-done | bytes 196624 | tf_op jit(solution)/shard_map/while/body/eval_jaxpr/psum | solution.py:12
  661.9 5.8 fusion.36
  667.9 66.3 %pmax.13 = f32[64]{0:T(128)S(1)} all-reduce(f32[64]{0:T(128)S(1)} %max.11), channel_id=1, replica_groups=mesh['wide'=16,'narrow'=8] {'wide','narrow'}, use_global_device_ids=true, to_apply=%region_11.11 | all-reduce | flops 64 | bytes 512 | tf_op jit(solution)/shard_map/while/body/eval_jaxpr/pmax | solution.py:107
  734.2 1.3 exponential_reduce_fusion.2
  735.7 62.5 %all-reduce.2 = (f32[64]{0:T(128)S(1)}, f32[64]{0:T(128)S(1)}) all-reduce(f32[64]{0:T(128)S(1)} %add.187, f32[64]{0:T(128)S(1)} %add.188), channel_id=1, replica_groups=mesh['wide'=16,'narrow'=8] {'wide','narrow'}, use_global_device_ids=true, to_apply=%region_18.18 | all-reduce | flops 128 | bytes 1024 | tf_op jit(solution)/shard_map/while/body/eval_jaxpr/psum | solution.py:112
  799.5 1.3 dynamic_slice.21
  802.2 11.2 %psum.59 = s32[64]{0:T(128)S(1)} all-reduce(s32[64]{0:T(128)S(1)} %fusion.37), channel_id=1, replica_groups=mesh['wide'=16,'narrow'=8] {'wide'}, use_global_device_ids=true, to_apply=%region_15.15 | all-reduce | flops 64 | bytes 512 | tf_op jit(solution)/shard_map/while/body/eval_jaxpr/psum | solution.py:12
  813.4 68.9 %all-reduce.8.cloned.1.call-done = bf16[64,1536]{1,0:T(8,128)(2,1)} async-done(((bf16[64,1536]{1,0:T(8,128)(2,1)}), bf16[64,1536]{1,0:T(8,128)(2,1)}) %all-reduce.8.cloned.1.call-update) | async-done | bytes 196624 | tf_op jit(solution)/shard_map/while/body/eval_jaxpr/psum | solution.py:12
  882.4 5.8 fusion.36
  888.4 66.3 %pmax.13 = f32[64]{0:T(128)S(1)} all-reduce(f32[64]{0:T(128)S(1)} %max.11), channel_id=1, replica_groups=mesh['wide'=16,'narrow'=8] {'wide','narrow'}, use_global_device_ids=true, to_apply=%region_11.11 | all-reduce | flops 64 | bytes 512 | tf_op jit(solution)/shard_map/while/body/eval_jaxpr/pmax | solution.py:107
  954.7 1.3 exponential_reduce_fusion.2
  956.2 62.5 %all-reduce.2 = (f32[64]{0:T(128)S(1)}, f32[64]{0:T(128)S(1)}) all-reduce(f32[64]{0:T(128)S(1)} %add.187, f32[64]{0:T(128)S(1)} %add.188), channel_id=1, replica_groups=mesh['wide'=16,'narrow'=8] {'wide','narrow'}, use_global_device_ids=true, to_apply=%region_18.18 | all-reduce | flops 128 | bytes 1024 | tf_op jit(solution)/shard_map/while/body/eval_jaxpr/psum | solution.py:112
  (86 shorter events, 12.6 us)
Async XLA Ops:
  7.2 10.1 copy-start
  7.2 103.3 %all-reduce.6.cloned.1.call-start = ((), (), s32[]{:S(2)}) async-start(), calls=%async_computation.4 | async-start | bytes 196608 | tf_op jit(solution)/shard_map/psum | solution.py:49
  7.2 5.8 copy-start.1
  14.5 2.7 copy-start.2
  26.9 23.8 %copy-start.4 = (s32[16]{0:T(128)S(1)}, s32[16]{0:T(128)}, u32[]{:S(2)}) copy-start(s32[16]{0:T(128)} %param.19) | copy-start | bytes 196
  50.9 26.9 %copy-start.5 = (s32[16]{0:T(128)}, s32[16]{0:T(128)S(1)}, u32[]{:S(2)}) copy-start(s32[16]{0:T(128)S(1)} %multiply_add_fusion.1) | copy-start | bytes 196
  51.8 13.9 %all-to-all-start.2 = ((s32[16,2,1]{1,2,0:T(1,128)}), s32[16,2,1]{1,2,0:T(1,128)}, u32[]{:S(2)}, u32[]{:S(2)}) async-start(s32[16,2,1]{1,2,0:T(1,128)} %bitcast.4), calls=%async_computation.2 | async-start | bytes 16384 | tf_op jit(solution)/shard_map/all_to_all | solution.py:74
  65.7 12.2 %all-to-all-start.3 = ((s32[16,2,1]{1,2,0:T(1,128)}), s32[16,2,1]{1,2,0:T(1,128)S(1)}, u32[]{:S(2)}, u32[]{:S(2)}) async-start(s32[16,2,1]{1,2,0:T(1,128)} %all-to-all-done.2), calls=%async_computation.3 | async-start | bytes 16384 | tf_op jit(solution)/shard_map/all_to_all | solution.py:73
  113.1 13.1 %all-to-all-start = ((bf16[16,2,192]{2,1,0:T(2,128)(2,1)}), bf16[16,2,192]{2,1,0:T(2,128)(2,1)}, u32[]{:S(2)}, u32[]{:S(2)}) async-start(bf16[16,2,192]{2,1,0:T(2,128)(2,1)} %reshape.84), calls=%async_computation | async-start | bytes 32768 | tf_op jit(solution)/shard_map/all_to_all | solution.py:67
  126.2 11.9 %all-to-all-start.1 = ((bf16[16,2,192]{2,1,0:T(2,128)(2,1)}), bf16[16,2,192]{2,1,0:T(2,128)(2,1)S(1)}, u32[]{:S(2)}, u32[]{:S(2)}) async-start(bf16[16,2,192]{2,1,0:T(2,128)(2,1)} %all-to-all-done), calls=%async_computation.1 | async-start | bytes 32768 | tf_op jit(solution)/shard_map/all_to_all | solution.py:66
  138.8 81.8 %all-reduce.8.cloned.1.call-start = ((), (), s32[]{:S(2)}) async-start(), calls=%async_computation.5 | async-start | bytes 393216 | tf_op jit(solution)/shard_map/while/body/eval_jaxpr/psum | solution.py:12
  220.6 5.8 copy-start.3
  358.2 83.2 %all-reduce.8.cloned.1.call-start = ((), (), s32[]{:S(2)}) async-start(), calls=%async_computation.5 | async-start | bytes 393216 | tf_op jit(solution)/shard_map/while/body/eval_jaxpr/psum | solution.py:12
  441.4 5.8 copy-start.3
  579.0 82.9 %all-reduce.8.cloned.1.call-start = ((), (), s32[]{:S(2)}) async-start(), calls=%async_computation.5 | async-start | bytes 393216 | tf_op jit(solution)/shard_map/while/body/eval_jaxpr/psum | solution.py:12
  661.9 5.8 copy-start.3
  799.5 82.9 %all-reduce.8.cloned.1.call-start = ((), (), s32[]{:S(2)}) async-start(), calls=%async_computation.5 | async-start | bytes 393216 | tf_op jit(solution)/shard_map/while/body/eval_jaxpr/psum | solution.py:12
  882.4 5.8 copy-start.3
Sparse Core Ops, SparseCore 0:
  50.9 59.5 all-reduce.5
  142.8 77.7 all-reduce.7
  362.2 79.1 all-reduce.7
  582.8 79.0 all-reduce.7
  803.2 79.1 all-reduce.7
where the time goes:
time: 1030 us
  blocking collectives  556 us (54%)
  waiting for transfers between devices  330 us (32%)
  matrix products  56.9 us (6%)
  starting transfers between devices  29 us (3%)
  other arithmetic  22 us (2%)
  local copies, waits for them, and re-layouts  15.6 us (2%)
  between operations  13.8 us (1%)
    psum x4, waiting for transfers between devices, spread(): return lax.psum(jnp.where(mine, x, jnp.zeros_like(x)), axis)  278 us
    pmax x4, blocking collectives, score_rows(): largest = lax.pmax(local_max, ('wide', 'narrow'))  265 us
    psum x4, blocking collectives, score_rows(): total, picked = lax.psum((local_total, local_positive), ('wide', 'narrow'))  250 us
    psum x4, blocking collectives, spread(): return lax.psum(jnp.where(mine, x, jnp.zeros_like(x)), axis)  40.4 us
    psum x1, waiting for transfers between devices, local(): pooled = lax.psum(pooled_part, 'narrow') + token_mean  32.4 us
    dot_general x4, matrix products, score_rows(): lax.dot_general(block, slab_old, contract, preferred_element_type=jnp.flo...  23.3 us
    dot_general x1, matrix products, local(): jnp.dot(hidden, down_weight, preferred_element_type=jnp.float32)  22.3 us
  transfers between devices with their start and end apart: 9, of which 9 were waited for; matrix products, arithmetic and copies ran while one was open for 0% of the time, Pallas kernels for 0%

commit v1 on v0

--- a/solution.py
+++ b/solution.py
@@ -5,6 +5,11 @@
 from jax.sharding import PartitionSpec as P
 
 EPS = 1e-06
+
+
+def one_after_other(array, axis_one, axis_two):
+    partial = lax.psum(array, axis_one)
+    return lax.psum(partial, axis_two)
 
 
 def spread(x, axis, root):
@@ -109,7 +114,7 @@
         local_total = local_total + jnp.sum(
             jnp.where(valid, jnp.exp(new_scores - largest[:, None]), 0.0), axis=1
         )
-        total, picked = lax.psum((local_total, local_positive), ("wide", "narrow"))
+        total, picked = one_after_other((local_total, local_positive), "wide", "narrow")
         return largest + jnp.log(total) - picked
 
     def step_body(step, losses):

time: 1030 us -> 969 us (0.941)
  blocking collectives: 556 us -> 498 us
    psum x4 -> x8, blocking collectives: 250 us -> 202 us  [the longest x4 124 us: one_after_other(): partial = lax.psum(array, axis_one)]
where the time goes in v1:
time: 969 us; the launch traced here: 967 us
  blocking collectives  498 us (51%)
  waiting for transfers between devices  329 us (34%)
  matrix products  56.9 us (6%)
  starting transfers between devices  29 us (3%)
  other arithmetic  22 us (2%)
  local copies, waits for them, and re-layouts  15.6 us (2%)
  between operations  13.8 us (1%)
    psum x4, waiting for transfers between devices, spread(): return lax.psum(jnp.where(mine, x, jnp.zeros_like(x)), axis)  276 us
    pmax x4, blocking collectives, score_rows(): largest = lax.pmax(local_max, ('wide', 'narrow'))  265 us
    psum x4, blocking collectives, one_after_other(): partial = lax.psum(array, axis_one)  124 us
    psum x4, blocking collectives, one_after_other(): return lax.psum(partial, axis_two)  77.7 us
    psum x1, waiting for transfers between devices, local(): pooled = lax.psum(pooled_part, 'narrow') + token_mean  32.4 us
    psum x4, blocking collectives, spread(): return lax.psum(jnp.where(mine, x, jnp.zeros_like(x)), axis)  30.4 us
    dot_general x4, matrix products, score_rows(): lax.dot_general(block, slab_old, contract, preferred_element_type=jnp.flo...  23.3 us
    dot_general x1, matrix products, local(): jnp.dot(hidden, down_weight, preferred_element_type=jnp.float32)  22.3 us
  transfers between devices with their start and end apart: 9, of which 9 were waited for; matrix products, arithmetic and copies ran while one was open for 0% of the time, Pallas kernels for 0%

profile of v1, /device:TPU:1, one launch (start us, length us, event | category | flops | bytes accessed | tf_op | source)
XLA Modules:
  0.0 967.3 jit_solution(880093934497975516)
XLA Ops:
  8.1 4.9 convert_reduce_fusion
  13.0 1.5 fusion.5
  14.5 2.7 copy-done.2
  17.2 9.7 %fusion.16 = f32[2048,1120]{0,1:T(8,128)} fusion(bf16[2048,1536]{1,0:T(8,128)(2,1)S(1)} %bitcast.50, bf16[1536,1120]{0,1:T(8,128)(2,1)S(1)} %copy-done), kind=kOutput, calls=%fused_computation.49 | convolution fusion | flops 7046430720 | bytes 18907136 | tf_op jit(solution)/shard_map/dot_general | solution.py:47
  26.9 22.3 %bitcast_reduce_fusion = f32[16,1536]{1,0:T(8,128)} fusion(bf16[1120,1536]{1,0:T(8,128)(2,1)} %param.17, bf16[2048,1536]{1,0:T(8,128)(2,1)} %bitcast.51, bf16[1536,1120]{0,1:T(8,128)(2,1)} %param.16, f32[2048,1120]{0,1:T(8,128)} %fusion.16), kind=kOutput, calls=%fused_computation.19 | convolution fusion | flops 14109745152 | bytes 22446080 | tf_op jit(solution)/shard_map/dot_general | solution.py:50
  49.2 1.5 broadcast_multiply_fusion
  51.8 7.6 all-to-all-start.2
  59.4 1.4 dynamic-slice_convert_fusion
  60.8 4.9 all-to-all-done.2
  65.7 7.6 all-to-all-start.3
  73.2 4.6 all-to-all-done.3
  78.1 32.4 %all-reduce.9.cloned.1.call-done = f32[16,1536]{1,0:T(8,128)} async-done(((f32[16,1536]{1,0:T(8,128)}), f32[16,1536]{1,0:T(8,128)}) %all-reduce.9.cloned.1.call-update) | async-done | bytes 98320 | tf_op jit(solution)/shard_map/psum | solution.py:54
  113.1 6.6 all-to-all-start
  119.8 6.3 all-to-all-done
  126.2 7.2 all-to-all-start.1
  133.6 4.4 all-to-all-done.1
  138.8 822.0 %while.14 = (s32[]{:T(128)}, f32[4,64]{1,0:T(4,128)}, s32[4]{0:T(128)}, bf16[1,64,1536]{2,1,0:T(8,128)(2,1)}, bf16[2048,1536]{1,0:T(8,128)(2,1)}, /*index=5*/pre...) while((s32[]{:T(128)}, f32[4,64]{1,0:T(4,128)}, ...), condition=%wide.region_21.22_spmd.clone, body=%wide.region_7.21_spmd.clone.sunk | while | flops 404558720 | bytes 10133544 | solution.py:127
  138.9 1.3 dynamic_slice.21
  141.6 9.3 psum.83
  150.9 69.7 %all-reduce.11.cloned.1.call-done = bf16[64,1536]{1,0:T(8,128)(2,1)} async-done(((bf16[64,1536]{1,0:T(8,128)(2,1)}), bf16[64,1536]{1,0:T(8,128)(2,1)}) %all-reduce.11.cloned.1.call-update) | async-done | bytes 196624 | tf_op jit(solution)/shard_map/while/body/eval_jaxpr/psum | solution.py:17
  220.6 5.8 fusion.36
  226.6 66.3 %pmax.13 = f32[64]{0:T(128)S(1)} all-reduce(f32[64]{0:T(128)S(1)} %max.11), channel_id=1, replica_groups=mesh['wide'=16,'narrow'=8] {'wide','narrow'}, use_global_device_ids=true, to_apply=%region_11.11 | all-reduce | flops 64 | bytes 512 | tf_op jit(solution)/shard_map/while/body/eval_jaxpr/pmax | solution.py:112
  293.0 1.3 exponential_reduce_fusion.2
  294.4 31.1 %all-reduce.4 = (f32[64]{0:T(128)S(1)}, f32[64]{0:T(128)S(1)}) all-reduce(f32[64]{0:T(128)S(1)} %add.191, f32[64]{0:T(128)S(1)} %add.192), channel_id=1, replica_groups=mesh['wide'=16,'narrow'=8] {'wide'}, use_global_device_ids=true, to_apply=%region_19.19 | all-reduce | flops 128 | bytes 1024 | tf_op jit(solution)/shard_map/while/body/eval_jaxpr/psum | solution.py:11
  325.5 19.4 %all-reduce.5 = (f32[64]{0:T(128)S(1)}, f32[64]{0:T(128)S(1)}) all-reduce(f32[64]{0:T(128)S(1)} %get-tuple-element.312, f32[64]{0:T(128)S(1)} %get-tuple-element.313), channel_id=1, replica_groups=mesh['wide'=16,'narrow'=8] {'narrow'}, use_global_device_ids=true, to_apply=%region_20.20 | all-reduce | flops 128 | bytes 1024 | tf_op jit(solution)/shard_map/while/body/eval_jaxpr/psum | solution.py:12
  346.2 1.3 dynamic_slice.21
  349.0 6.9 psum.83
  355.9 69.7 %all-reduce.11.cloned.1.call-done = bf16[64,1536]{1,0:T(8,128)(2,1)} async-done(((bf16[64,1536]{1,0:T(8,128)(2,1)}), bf16[64,1536]{1,0:T(8,128)(2,1)}) %all-reduce.11.cloned.1.call-update) | async-done | bytes 196624 | tf_op jit(solution)/shard_map/while/body/eval_jaxpr/psum | solution.py:17
  425.6 5.8 fusion.36
  431.6 66.3 %pmax.13 = f32[64]{0:T(128)S(1)} all-reduce(f32[64]{0:T(128)S(1)} %max.11), channel_id=1, replica_groups=mesh['wide'=16,'narrow'=8] {'wide','narrow'}, use_global_device_ids=true, to_apply=%region_11.11 | all-reduce | flops 64 | bytes 512 | tf_op jit(solution)/shard_map/while/body/eval_jaxpr/pmax | solution.py:112
  498.0 1.3 exponential_reduce_fusion.2
  499.4 31.1 %all-reduce.4 = (f32[64]{0:T(128)S(1)}, f32[64]{0:T(128)S(1)}) all-reduce(f32[64]{0:T(128)S(1)} %add.191, f32[64]{0:T(128)S(1)} %add.192), channel_id=1, replica_groups=mesh['wide'=16,'narrow'=8] {'wide'}, use_global_device_ids=true, to_apply=%region_19.19 | all-reduce | flops 128 | bytes 1024 | tf_op jit(solution)/shard_map/while/body/eval_jaxpr/psum | solution.py:11
  530.5 19.4 %all-reduce.5 = (f32[64]{0:T(128)S(1)}, f32[64]{0:T(128)S(1)}) all-reduce(f32[64]{0:T(128)S(1)} %get-tuple-element.312, f32[64]{0:T(128)S(1)} %get-tuple-element.313), channel_id=1, replica_groups=mesh['wide'=16,'narrow'=8] {'narrow'}, use_global_device_ids=true, to_apply=%region_20.20 | all-reduce | flops 128 | bytes 1024 | tf_op jit(solution)/shard_map/while/body/eval_jaxpr/psum | solution.py:12
  553.2 1.6 select_bitcast_fusion.2
  555.6 5.4 psum.83
  561.0 69.5 %all-reduce.11.cloned.1.call-done = bf16[64,1536]{1,0:T(8,128)(2,1)} async-done(((bf16[64,1536]{1,0:T(8,128)(2,1)}), bf16[64,1536]{1,0:T(8,128)(2,1)}) %all-reduce.11.cloned.1.call-update) | async-done | bytes 196624 | tf_op jit(solution)/shard_map/while/body/eval_jaxpr/psum | solution.py:17
  630.4 5.8 fusion.36
  636.5 66.3 %pmax.13 = f32[64]{0:T(128)S(1)} all-reduce(f32[64]{0:T(128)S(1)} %max.11), channel_id=1, replica_groups=mesh['wide'=16,'narrow'=8] {'wide','narrow'}, use_global_device_ids=true, to_apply=%region_11.11 | all-reduce | flops 64 | bytes 512 | tf_op jit(solution)/shard_map/while/body/eval_jaxpr/pmax | solution.py:112
  702.8 1.3 exponential_reduce_fusion.2
  704.2 31.1 %all-reduce.4 = (f32[64]{0:T(128)S(1)}, f32[64]{0:T(128)S(1)}) all-reduce(f32[64]{0:T(128)S(1)} %add.191, f32[64]{0:T(128)S(1)} %add.192), channel_id=1, replica_groups=mesh['wide'=16,'narrow'=8] {'wide'}, use_global_device_ids=true, to_apply=%region_19.19 | all-reduce | flops 128 | bytes 1024 | tf_op jit(solution)/shard_map/while/body/eval_jaxpr/psum | solution.py:11
  735.3 19.4 %all-reduce.5 = (f32[64]{0:T(128)S(1)}, f32[64]{0:T(128)S(1)}) all-reduce(f32[64]{0:T(128)S(1)} %get-tuple-element.312, f32[64]{0:T(128)S(1)} %get-tuple-element.313), channel_id=1, replica_groups=mesh['wide'=16,'narrow'=8] {'narrow'}, use_global_device_ids=true, to_apply=%region_20.20 | all-reduce | flops 128 | bytes 1024 | tf_op jit(solution)/shard_map/while/body/eval_jaxpr/psum | solution.py:12
  758.8 8.8 psum.83
  767.6 67.5 %all-reduce.11.cloned.1.call-done = bf16[64,1536]{1,0:T(8,128)(2,1)} async-done(((bf16[64,1536]{1,0:T(8,128)(2,1)}), bf16[64,1536]{1,0:T(8,128)(2,1)}) %all-reduce.11.cloned.1.call-update) | async-done | bytes 196624 | tf_op jit(solution)/shard_map/while/body/eval_jaxpr/psum | solution.py:17
  835.2 5.8 fusion.36
  841.2 66.3 %pmax.13 = f32[64]{0:T(128)S(1)} all-reduce(f32[64]{0:T(128)S(1)} %max.11), channel_id=1, replica_groups=mesh['wide'=16,'narrow'=8] {'wide','narrow'}, use_global_device_ids=true, to_apply=%region_11.11 | all-reduce | flops 64 | bytes 512 | tf_op jit(solution)/shard_map/while/body/eval_jaxpr/pmax | solution.py:112
  907.5 1.3 exponential_reduce_fusion.2
  909.0 31.1 %all-reduce.4 = (f32[64]{0:T(128)S(1)}, f32[64]{0:T(128)S(1)}) all-reduce(f32[64]{0:T(128)S(1)} %add.191, f32[64]{0:T(128)S(1)} %add.192), channel_id=1, replica_groups=mesh['wide'=16,'narrow'=8] {'wide'}, use_global_device_ids=true, to_apply=%region_19.19 | all-reduce | flops 128 | bytes 1024 | tf_op jit(solution)/shard_map/while/body/eval_jaxpr/psum | solution.py:11
  940.1 19.4 %all-reduce.5 = (f32[64]{0:T(128)S(1)}, f32[64]{0:T(128)S(1)}) all-reduce(f32[64]{0:T(128)S(1)} %get-tuple-element.312, f32[64]{0:T(128)S(1)} %get-tuple-element.313), channel_id=1, replica_groups=mesh['wide'=16,'narrow'=8] {'narrow'}, use_global_device_ids=true, to_apply=%region_20.20 | all-reduce | flops 128 | bytes 1024 | tf_op jit(solution)/shard_map/while/body/eval_jaxpr/psum | solution.py:12
  (90 shorter events, 17.8 us)
Async XLA Ops:
  7.2 10.1 %copy-start = (bf16[1536,1120]{0,1:T(8,128)(2,1)S(1)}, bf16[1536,1120]{0,1:T(8,128)(2,1)}, u32[]{:S(2)}) copy-start(bf16[1536,1120]{0,1:T(8,128)(2,1)} %param.15) | copy-start | bytes 10321924
  7.2 103.3 %all-reduce.9.cloned.1.call-start = ((), (), s32[]{:S(2)}) async-start(), calls=%async_computation.4 | async-start | bytes 196608 | tf_op jit(solution)/shard_map/psum | solution.py:54
  7.2 5.8 copy-start.1
  14.5 2.7 copy-start.2
  26.9 23.8 %copy-start.4 = (s32[16]{0:T(128)S(1)}, s32[16]{0:T(128)}, u32[]{:S(2)}) copy-start(s32[16]{0:T(128)} %param.19) | copy-start | bytes 196
  50.9 26.9 %copy-start.5 = (s32[16]{0:T(128)}, s32[16]{0:T(128)S(1)}, u32[]{:S(2)}) copy-start(s32[16]{0:T(128)S(1)} %multiply_add_fusion.1) | copy-start | bytes 196
  51.8 13.9 %all-to-all-start.2 = ((s32[16,2,1]{1,2,0:T(1,128)}), s32[16,2,1]{1,2,0:T(1,128)}, u32[]{:S(2)}, u32[]{:S(2)}) async-start(s32[16,2,1]{1,2,0:T(1,128)} %bitcast.4), calls=%async_computation.2 | async-start | bytes 16384 | tf_op jit(solution)/shard_map/all_to_all | solution.py:79
  65.7 12.2 %all-to-all-start.3 = ((s32[16,2,1]{1,2,0:T(1,128)}), s32[16,2,1]{1,2,0:T(1,128)S(1)}, u32[]{:S(2)}, u32[]{:S(2)}) async-start(s32[16,2,1]{1,2,0:T(1,128)} %all-to-all-done.2), calls=%async_computation.3 | async-start | bytes 16384 | tf_op jit(solution)/shard_map/all_to_all | solution.py:78
  113.1 13.1 %all-to-all-start = ((bf16[16,2,192]{2,1,0:T(2,128)(2,1)}), bf16[16,2,192]{2,1,0:T(2,128)(2,1)}, u32[]{:S(2)}, u32[]{:S(2)}) async-start(bf16[16,2,192]{2,1,0:T(2,128)(2,1)} %reshape.84), calls=%async_computation | async-start | bytes 32768 | tf_op jit(solution)/shard_map/all_to_all | solution.py:72
  126.2 11.9 %all-to-all-start.1 = ((bf16[16,2,192]{2,1,0:T(2,128)(2,1)}), bf16[16,2,192]{2,1,0:T(2,128)(2,1)S(1)}, u32[]{:S(2)}, u32[]{:S(2)}) async-start(bf16[16,2,192]{2,1,0:T(2,128)(2,1)} %all-to-all-done), calls=%async_computation.1 | async-start | bytes 32768 | tf_op jit(solution)/shard_map/all_to_all | solution.py:71
  138.8 81.8 %all-reduce.11.cloned.1.call-start = ((), (), s32[]{:S(2)}) async-start(), calls=%async_computation.5 | async-start | bytes 393216 | tf_op jit(solution)/shard_map/while/body/eval_jaxpr/psum | solution.py:17
  220.6 5.8 copy-start.3
  346.2 79.4 %all-reduce.11.cloned.1.call-start = ((), (), s32[]{:S(2)}) async-start(), calls=%async_computation.5 | async-start | bytes 393216 | tf_op jit(solution)/shard_map/while/body/eval_jaxpr/psum | solution.py:17
  425.6 5.8 copy-start.3
  551.2 79.2 %all-reduce.11.cloned.1.call-start = ((), (), s32[]{:S(2)}) async-start(), calls=%async_computation.5 | async-start | bytes 393216 | tf_op jit(solution)/shard_map/while/body/eval_jaxpr/psum | solution.py:17
  630.4 5.8 copy-start.3
  756.1 79.1 %all-reduce.11.cloned.1.call-start = ((), (), s32[]{:S(2)}) async-start(), calls=%async_computation.5 | async-start | bytes 393216 | tf_op jit(solution)/shard_map/while/body/eval_jaxpr/psum | solution.py:17
  835.2 5.8 copy-start.3
Sparse Core Ops, SparseCore 0:
  50.9 59.5 all-reduce.8
  142.8 77.7 all-reduce.10
  350.2 75.3 all-reduce.10
  555.0 75.3 all-reduce.10
  759.7 75.3 all-reduce.10
